TPU v7x, 32 devices: a whole 2x2x4 slice. The times are simulated.
32 devices in a mesh: node: 8 (over z, x), feat: 4 (over y, core).
Axes of the slice: x: 2, y: 2, z: 4, core: 2. Of those that a mesh axis runs over, the one named last changes fastest.
Arguments:
- feature_table: bfloat16 [8192, 2048], P('node', 'feat'), may hold values from -6 to 6
- hub_table: bfloat16 [32, 2048], P('node', 'feat'), may hold values from -6 to 6
- first_self: bfloat16 [2048, 2048], P('feat'), may hold values from -0.125 to 0.125
- first_pooled: bfloat16 [2048, 2048], P('feat'), may hold values from -0.125 to 0.125
- second_self: bfloat16 [2048, 256], P('feat'), may hold values from -0.125 to 0.125
- second_pooled: bfloat16 [2048, 256], P('feat'), may hold values from -0.125 to 0.125
- first_lists: int32 [3072, 10], P('node'), may hold values from 0 to 8223, as said below
- first_counts: int32 [3072], P('node'), may hold values from 1 to 10
- second_lists: int32 [2048, 5], P('node'), may hold values from 0 to 3071, as said below
- second_counts: int32 [2048], P('node'), may hold values from 1 to 5
Outputs:
- embedding: bfloat16 [2048, 256], P(('node', 'feat'))
Inputs may be any that keep to these rules, and one draw needn't show every extreme that they name: `first_lists`: an entry below 8192 names a row of feature_table, held by node shard (entry // 1024); an entry v of 8192 or more names hub clip v - 8192, owned by node shard (v - 8192) // 4. Slots at or beyond a clip's count are padding and still hold such entries. Of the 3840 entries of one node shard's rows, padding included, at most 480 name feature rows held by any one node shard; in every draw one node shard is named exactly 480 times by the rows of every node shard. `second_lists`: entries name frontier clips, held by node shard (entry // 384). Of the 1280 entries of one node shard's rows, padding included, exactly 160 name frontier clips of each node shard.
All inputs are finite; a program needn't handle non-finite values.
Results may differ from a plain program's by a relative error of at most 0.0052.
Values may be sent and summed in bfloat16 or wider, within the bound.
A program may use at most 64 MiB of HBM per device.

v0:
```python
import jax
import jax.numpy as jnp
from jax import lax
from jax.sharding import PartitionSpec as P


def count_matrix(local, width):
    columns = jnp.arange(width, dtype=jnp.int32)[None, :]
    total = jnp.zeros((local.shape[0], width), jnp.float32)
    for k in range(local.shape[1]):
        total = total + (local[:, k : k + 1] == columns).astype(jnp.float32)
    return total.astype(jnp.bfloat16)


def body(
    feature_table,
    hub_table,
    first_self,
    first_pooled,
    second_self,
    second_pooled,
    first_lists,
    first_counts,
    second_lists,
    second_counts,
):
    shards = lax.axis_size("node")
    me = lax.axis_index("node")
    rows_here = feature_table.shape[0]
    hubs_here = hub_table.shape[0]
    front_here, fan_one = first_lists.shape
    targets_here, fan_two = second_lists.shape
    total_rows = rows_here * shards
    slots_one = jnp.arange(fan_one, dtype=jnp.int32)[None, :]
    slots_two = jnp.arange(fan_two, dtype=jnp.int32)[None, :]
    lists_one = jnp.where(slots_one < first_counts[:, None], first_lists, -1)
    lists_two = jnp.where(slots_two < second_counts[:, None], second_lists, -1)
    packed = jnp.concatenate([lists_one.reshape(-1), lists_two.reshape(-1), second_counts]).reshape(
        1, -1
    )
    everyone = lax.all_gather(packed, "node", axis=0, tiled=True)
    cut_one = front_here * fan_one
    cut_two = cut_one + targets_here * fan_two
    all_one = everyone[:, :cut_one].reshape(shards * front_here, fan_one)
    all_two = everyone[:, cut_one:cut_two].reshape(shards * targets_here, fan_two)
    all_counts = everyone[:, cut_two:].reshape(shards * targets_here, 1)
    feature_at = all_one - me * rows_here
    hub_at = all_one - total_rows - me * hubs_here
    local_one = jnp.where(
        (feature_at >= 0) & (feature_at < rows_here) & (all_one >= 0),
        feature_at,
        jnp.where((hub_at >= 0) & (hub_at < hubs_here), hub_at + rows_here, -1),
    )
    combined = jnp.concatenate([feature_table, hub_table], axis=0)
    matrix_one = count_matrix(local_one, rows_here + hubs_here)
    sums = jnp.dot(matrix_one, combined, preferred_element_type=jnp.float32)
    sums = lax.psum_scatter(sums.astype(jnp.bfloat16), "node", scatter_dimension=0, tiled=True)
    first_mean = (sums.astype(jnp.float32) / first_counts[:, None].astype(jnp.float32)).astype(
        jnp.bfloat16
    )
    part = jnp.dot(feature_table[:front_here], first_self, preferred_element_type=jnp.float32)
    part = part + jnp.dot(first_mean, first_pooled, preferred_element_type=jnp.float32)
    hidden = jax.nn.relu(
        lax.psum_scatter(part.astype(jnp.bfloat16), "feat", scatter_dimension=1, tiled=True)
    )
    projected = jnp.dot(hidden, second_pooled, preferred_element_type=jnp.float32)
    own = jnp.dot(hidden[:targets_here], second_self, preferred_element_type=jnp.float32)
    local_two = jnp.where(all_two >= 0, all_two - me * front_here, -1)
    matrix_two = count_matrix(local_two, front_here)
    mixed = jnp.dot(
        matrix_two, projected.astype(jnp.bfloat16), preferred_element_type=jnp.float32
    ) / all_counts.astype(jnp.float32)
    here = lax.dynamic_slice_in_dim(mixed, me * targets_here, targets_here, 0)
    mixed = lax.dynamic_update_slice_in_dim(mixed, here + own, me * targets_here, 0)
    mixed = lax.psum_scatter(mixed, ("node", "feat"), scatter_dimension=0, tiled=True)
    scale = lax.rsqrt(jnp.mean(mixed * mixed, axis=1, keepdims=True) + 1e-06)
    return (mixed * scale).astype(jnp.bfloat16)


def solution(mesh):
    return jax.shard_map(
        body,
        mesh=mesh,
        in_specs=(
            P("node", "feat"),
            P("node", "feat"),
            P("feat", None),
            P("feat", None),
            P("feat", None),
            P("feat", None),
            P("node", None),
            P("node"),
            P("node", None),
            P("node"),
        ),
        out_specs=P(("node", "feat"), None),
        check_vma=False,
    )
```

profile of v0, /device:TPU:0, one launch (start us, length us, event | category | flops | bytes accessed | tf_op | source)
XLA Modules:
  0.0 341.4 jit_solution(16329909199386390386)
XLA Ops:
  6.5 0.9 fusion.27
  7.4 0.1 copy.16
  7.5 0.2 reshape.54
  7.7 0.7 fusion.25
  8.5 0.1 copy.15
  8.6 0.1 reshape.53
  8.8 0.7 pad_add_fusion
  9.5 32.4 %all-gather.1 = s32[8,1,5376]{2,1,0:T(1,128)S(1)} all-gather(s32[1,1,5376]{2,1,0:T(1,128)S(1)} %reshape.59), channel_id=2, replica_groups=mesh['node'=8,'feat'=4] {'node'}, dimensions={0}, use_global_device_ids=true | all-gather | bytes 193536 | tf_op jit(solution)/shard_map/all_gather | solution.py:41
  42.0 1.8 ge.24
  43.8 2.8 reshape.57
  46.6 2.8 sub.31
  49.4 2.3 and_select_fusion
  51.7 7.9 %slice_reduce_fusion.9 = (s32[3072]{0:T(1024)S(1)}, s32[3072]{0:T(1024)S(1)}, s32[3072]{0:T(1024)S(1)}, s32[3072]{0:T(1024)S(1)}, s32[3072]{0:T(1024)S(1)}, /*in...) fusion(s32[3072,10]{1,0:T(8,128)S(1)} %and_select_fusion), kind=kLoop, calls=%fused_computation.40 | loop fusion | bytes 245760 | tf_op jit(solution)/shard_map/slice | solution.py:11
  59.7 19.4 %fusion.11 = bf16[3072,512]{1,0:T(8,128)(2,1)} fusion(s32[3072]{0:T(1024)S(1)} %get-tuple-element.6, s32[3072]{0:T(1024)S(1)} %get-tuple-element.7, s32[3072]{0:T(1024)S(1)} %get-tuple-element.8, s32[3072]{0:T(1024)S(1)} %get-tuple-element.9, s32[3072]{0:T(1024)S(1)} %get-tuple-element.10, s32[3072]{0:T(1024)S(1)} %get-tuple-element.11, ...), kind=kOutput, calls=%fused_computation.22 | convolution fusion | flops 3332227072 | bytes 4321280 | tf_op jit(solution)/shard_map/dot_general | solution.py:56
  79.1 0.0 reduce-scatter.4.cloned.1.call-update
  79.1 0.0 reduce-scatter.6.cloned.1.call-start
  79.1 0.6 copy-done.3
  79.8 3.6 %fusion.22 = f32[384,2048]{1,0:T(8,128)} fusion(bf16[512,2048]{1,0:T(8,128)(2,1)S(1)} %copy-done, bf16[1024,512]{1,0:T(8,128)(2,1)} %param.10), kind=kOutput, calls=%fused_computation.60 | convolution fusion | flops 805306368 | bytes 5636096 | tf_op jit(solution)/shard_map/dot_general | solution.py:61
  83.4 71.1 %reduce-scatter.4.cloned.1.call-done = bf16[384,512]{1,0:T(8,128)(2,1)} async-done(((bf16[3072,512]{1,0:T(8,128)(2,1)}), bf16[384,512]{1,0:T(8,128)(2,1)}) %reduce-scatter.4.cloned.1.call-update) | async-done | bytes 393232 | tf_op jit(solution)/shard_map/reduce_scatter | solution.py:57
  154.5 4.8 %add_convert_fusion.4 = bf16[384,2048]{1,0:T(8,128)(2,1)} fusion(f32[384,2048]{1,0:T(8,128)} %fusion.22, bf16[512,2048]{1,0:T(8,128)(2,1)} %param.13, bf16[384,512]{1,0:T(8,128)(2,1)} %reduce-scatter.4.cloned.1.call-done, f32[384]{0:T(512)S(1)} %convert_element_type.103), kind=kOutput, calls=%fused_computation.23 | convolution fusion | flops 807469056 | bytes 7210496 | tf_op jit(solution)/shard_map/dot_general | solution.py:62
  159.3 0.0 reduce-scatter.6.cloned.1.call-update
  159.3 0.3 reduce-scatter.8.cloned.1.call-start
  159.7 0.9 select_n.30
  160.6 2.5 slice_reduce_fusion.14
  163.1 23.5 %reduce-scatter.6.cloned.1.call-done = bf16[384,512]{1,0:T(8,128)(2,1)} async-done(((bf16[384,2048]{1,0:T(8,128)(2,1)}), bf16[384,512]{1,0:T(8,128)(2,1)}) %reduce-scatter.6.cloned.1.call-update) | async-done | bytes 393232 | tf_op jit(solution)/shard_map/reduce_scatter | solution.py:64
  186.6 1.0 broadcast_maximum_fusion
  187.7 4.7 %convolution_divide_fusion = f32[2048,256]{1,0:T(8,128)} fusion(s32[2048]{0:T(1024)S(1)} %get-tuple-element.16, s32[2048]{0:T(1024)S(1)} %get-tuple-element.17, s32[2048]{0:T(1024)S(1)} %get-tuple-element.18, s32[2048]{0:T(1024)S(1)} %get-tuple-element.19, s32[2048]{0:T(1024)S(1)} %get-tuple-element.15, bf16[512,256]{1,0:T(8,128)(2,1)S(1)} %copy-done.4, ...), kind=kOutput, calls=%fused_computation.30 | convolution fusion | flops 515932160 | bytes 2801664 | tf_op jit(solution)/shard_map/dot_general | solution.py:70
  192.4 1.9 fusion.17
  194.2 0.0 reduce-scatter.8.cloned.1.call-update
  194.2 138.1 %reduce-scatter.8.cloned.1.call-done = f32[64,256]{1,0:T(8,128)} async-done(((f32[2048,256]{1,0:T(8,128)}), f32[64,256]{1,0:T(8,128)}) %reduce-scatter.8.cloned.1.call-update) | async-done | bytes 65552 | tf_op jit(solution)/shard_map/reduce_scatter | solution.py:75
  332.4 0.9 multiply_reduce_fusion
  333.3 1.5 multiply_convert_fusion
  (21 shorter events, 0.2 us)
Async XLA Ops:
  6.5 73.2 %copy-start = (bf16[512,2048]{1,0:T(8,128)(2,1)S(1)}, bf16[512,2048]{1,0:T(8,128)(2,1)}, u32[]{:S(2)}) copy-start(bf16[512,2048]{1,0:T(8,128)(2,1)} %param.12) | copy-start | bytes 6291460
  6.5 148.0 %reduce-scatter.4.cloned.1.call-start = ((), (), s32[]{:S(2)}) async-start(), calls=%async_computation.3 | async-start | bytes 3538944 | tf_op jit(solution)/shard_map/reduce_scatter | solution.py:57
  51.7 7.9 %copy-start.2 = (bf16[1024,512]{1,0:T(8,128)(2,1)S(1)}, bf16[1024,512]{1,0:T(8,128)(2,1)}, u32[]{:S(2)}) copy-start(bf16[1024,512]{1,0:T(8,128)(2,1)} %param.10) | copy-start | bytes 3145732
  51.7 7.9 %copy-start.5 = (bf16[4,512]{1,0:T(4,128)(2,1)S(1)}, bf16[4,512]{1,0:T(4,128)(2,1)}, u32[]{:S(2)}) copy-start(bf16[4,512]{1,0:T(4,128)(2,1)} %param.11) | copy-start | bytes 12292
  79.1 0.7 copy-start.3
  79.1 107.5 %reduce-scatter.6.cloned.1.call-start = ((), (), s32[]{:S(2)}) async-start(), calls=%async_computation.4 | async-start | bytes 1966080 | tf_op jit(solution)/shard_map/reduce_scatter | solution.py:64
  159.3 173.0 %reduce-scatter.8.cloned.1.call-start = ((), (), s32[]{:S(2)}) async-start(), calls=%async_computation.5 | async-start | bytes 2162688 | tf_op jit(solution)/shard_map/reduce_scatter | solution.py:75
  160.6 27.1 %copy-start.4 = (bf16[512,256]{1,0:T(8,128)(2,1)S(1)}, bf16[512,256]{1,0:T(8,128)(2,1)}, u32[]{:S(2)}) copy-start(bf16[512,256]{1,0:T(8,128)(2,1)} %param.15) | copy-start | bytes 786436
  187.6 4.7 %copy-start.1 = (bf16[512,256]{1,0:T(8,128)(2,1)S(1)}, bf16[512,256]{1,0:T(8,128)(2,1)}, u32[]{:S(2)}) copy-start(bf16[512,256]{1,0:T(8,128)(2,1)} %param.14) | copy-start | bytes 786436
Sparse Core Ops, SparseCore 0:
  79.2 75.2 reduce-scatter.3
  159.5 27.0 reduce-scatter.5
  194.4 137.9 reduce-scatter.7
where the time goes:
time: 342 us; the launch traced here: 341 us
  waiting for transfers between devices  233 us (68%)
  matrix products  34.4 us (10%)
  blocking collectives  32.4 us (9%)
  local copies, waits for them, and re-layouts  20 us (6%)
  between operations  13.3 us (4%)
  other arithmetic  8.17 us (2%)
    reduce_scatter x1, waiting for transfers between devices, body(): lax.psum_scatter(mixed, ('node', 'feat'), scatter_dimension=0, tiled=True)  138 us
    reduce_scatter x1, waiting for transfers between devices, body(): lax.psum_scatter(sums.astype(jnp.bfloat16), 'node', scatter_dimension=0,...  71.1 us
    all_gather x1, blocking collectives, body(): everyone = lax.all_gather(packed, 'node', axis=0, tiled=True)  32.4 us
    reduce_scatter x1, waiting for transfers between devices, body(): lax.psum_scatter(part.astype(jnp.bfloat16), 'feat', scatter_dimension=1,...  23.5 us
    dot_general x1, matrix products, body(): sums = jnp.dot(matrix_one, combined, preferred_element_type=jnp.float32)  19.4 us
    slice x2, local copies, waits for them, and re-layouts, count_matrix(): total = total + (local[:, k:k + 1] == columns).astype(jnp.float32)  10.4 us
  transfers between devices with their start and end apart: 3, of which 3 were waited for; matrix products, arithmetic and copies ran while one was open for 2% of the time, Pallas kernels for 0%

commit v1 on v0

--- a/solution.py
+++ b/solution.py
@@ -38,7 +38,15 @@
     packed = jnp.concatenate([lists_one.reshape(-1), lists_two.reshape(-1), second_counts]).reshape(
         1, -1
     )
-    everyone = lax.all_gather(packed, "node", axis=0, tiled=True)
+    ways, here_2, lap = (lax.axis_size("node"), lax.axis_index("node"), packed.shape[0])
+    line, have = (packed, 1)
+    while have < ways:
+        line = jnp.concatenate(
+            [line, lax.ppermute(line, "node", [(d, (d - have) % ways) for d in range(ways)])],
+            axis=0,
+        )
+        have = 2 * have
+    everyone = jnp.roll(line, here_2 * lap, axis=0)
     cut_one = front_here * fan_one
     cut_two = cut_one + targets_here * fan_two
     all_one = everyone[:, :cut_one].reshape(shards * front_here, fan_one)

time: 342 us -> 330 us (0.965)
  blocking collectives: 32.4 us -> 0 us
  waiting for transfers between devices: 233 us -> 245 us
  starting transfers between devices: 0.31 us -> 8.22 us
    all_gather x1 -> x0, blocking collectives: 32.4 us -> none  [body(): everyone = lax.all_gather(packed, 'node', axis=0, tiled=True)]
    ppermute x0 -> x3, waiting for transfers between devices: none -> 10.1 us  [body(): lax.ppermute(line, 'node', [(d, (d - have) % ways) for d in range(ways)])]
    ppermute x0 -> x3, starting transfers between devices: none -> 7.91 us  [body(): lax.ppermute(line, 'node', [(d, (d - have) % ways) for d in range(ways)])]
  transfers between devices with their start and end apart: 3 -> 6, of which waited for: 3 -> 6; matrix products, arithmetic and copies ran while one was open for 2% -> 2% of each run, Pallas kernels for 0% -> 0%
where the time goes in v1:
time: 330 us
  waiting for transfers between devices  245 us (74%)
  matrix products  34.4 us (10%)
  local copies, waits for them, and re-layouts  20.2 us (6%)
  between operations  13.3 us (4%)
  other arithmetic  8.45 us (3%)
  starting transfers between devices  8.22 us (2%)
    reduce_scatter x1, waiting for transfers between devices, body(): lax.psum_scatter(mixed, ('node', 'feat'), scatter_dimension=0, tiled=True)  139 us
    reduce_scatter x1, waiting for transfers between devices, body(): lax.psum_scatter(sums.astype(jnp.bfloat16), 'node', scatter_dimension=0,...  73 us
    reduce_scatter x1, waiting for transfers between devices, body(): lax.psum_scatter(part.astype(jnp.bfloat16), 'feat', scatter_dimension=1,...  23.4 us
    dot_general x1, matrix products, body(): sums = jnp.dot(matrix_one, combined, preferred_element_type=jnp.float32)  19.4 us
    slice x2, local copies, waits for them, and re-layouts, count_matrix(): total = total + (local[:, k:k + 1] == columns).astype(jnp.float32)  10.4 us
    ppermute x3, waiting for transfers between devices, body(): lax.ppermute(line, 'node', [(d, (d - have) % ways) for d in range(ways)])  10.1 us
    ppermute x3, starting transfers between devices, body(): lax.ppermute(line, 'node', [(d, (d - have) % ways) for d in range(ways)])  7.91 us
  transfers between devices with their start and end apart: 6, of which 6 were waited for; matrix products, arithmetic and copies ran while one was open for 2% of the time, Pallas kernels for 0%

profile of v1, /device:TPU:0, one launch (start us, length us, event | category | flops | bytes accessed | tf_op | source)
XLA Modules:
  0.0 329.8 jit_solution(3982592191175691346)
XLA Ops:
  6.5 0.9 fusion.27
  7.5 0.2 reshape.54
  7.7 0.7 fusion.25
  8.6 0.1 reshape.53
  8.8 0.7 pad_add_fusion.2
  9.5 6.1 %collective-permute-start = (s32[1,5376]{1,0:T(1,128)S(1)}, s32[1,5376]{1,0:T(1,128)S(1)}, u32[]{:S(2)}, u32[]{:S(2)}) collective-permute-start(s32[1,5376]{1,0:T(1,128)S(1)} %reshape.55), channel_id=1, source_target_pairs={{0,28},{4,0},{8,4},{12,8},{16,12},{20,16},{24,20},{28,24},{1,29},{... | collective-permute-start | bytes 64520 | tf_op jit(solution)/shard_map/ppermute | solution.py:45
  15.6 1.5 collective-permute-done
  17.1 1.4 collective-permute-start.1
  18.5 2.6 collective-permute-done.1
  21.2 0.4 collective-permute-start.2
  21.7 5.9 %collective-permute-done.2 = s32[4,5376]{1,0:T(4,128)S(1)} collective-permute-done((s32[4,5376]{1,0:T(4,128)S(1)}, s32[4,5376]{1,0:T(4,128)S(1)}, u32[]{:S(2)}, u32[]{:S(2)}) %collective-permute-start.2) | collective-permute-done | bytes 86048 | tf_op jit(solution)/shard_map/ppermute | solution.py:45
  27.6 0.3 concatenate.23
  27.9 1.8 ge.24
  29.8 2.8 reshape.57
  32.6 2.8 sub.36
  35.4 2.3 and_select_fusion
  37.7 7.9 %slice_reduce_fusion.9 = (s32[3072]{0:T(1024)S(1)}, s32[3072]{0:T(1024)S(1)}, s32[3072]{0:T(1024)S(1)}, s32[3072]{0:T(1024)S(1)}, s32[3072]{0:T(1024)S(1)}, /*in...) fusion(s32[3072,10]{1,0:T(8,128)S(1)} %and_select_fusion), kind=kLoop, calls=%fused_computation.40 | loop fusion | bytes 245760 | tf_op jit(solution)/shard_map/slice | solution.py:11
  45.6 19.4 %fusion.11 = bf16[3072,512]{1,0:T(8,128)(2,1)} fusion(s32[3072]{0:T(1024)S(1)} %get-tuple-element.6, s32[3072]{0:T(1024)S(1)} %get-tuple-element.7, s32[3072]{0:T(1024)S(1)} %get-tuple-element.8, s32[3072]{0:T(1024)S(1)} %get-tuple-element.9, s32[3072]{0:T(1024)S(1)} %get-tuple-element.10, s32[3072]{0:T(1024)S(1)} %get-tuple-element.11, ...), kind=kOutput, calls=%fused_computation.22 | convolution fusion | flops 3332227072 | bytes 4321280 | tf_op jit(solution)/shard_map/dot_general | solution.py:64
  65.1 0.6 copy-done.3
  65.7 3.6 %fusion.22 = f32[384,2048]{1,0:T(8,128)} fusion(bf16[512,2048]{1,0:T(8,128)(2,1)S(1)} %copy-done, bf16[1024,512]{1,0:T(8,128)(2,1)} %param.10), kind=kOutput, calls=%fused_computation.60 | convolution fusion | flops 805306368 | bytes 5636096 | tf_op jit(solution)/shard_map/dot_general | solution.py:69
  69.4 73.0 %reduce-scatter.4.cloned.1.call-done = bf16[384,512]{1,0:T(8,128)(2,1)} async-done(((bf16[3072,512]{1,0:T(8,128)(2,1)}), bf16[384,512]{1,0:T(8,128)(2,1)}) %reduce-scatter.4.cloned.1.call-update) | async-done | bytes 393232 | tf_op jit(solution)/shard_map/reduce_scatter | solution.py:65
  142.4 4.8 %add_convert_fusion.4 = bf16[384,2048]{1,0:T(8,128)(2,1)} fusion(f32[384,2048]{1,0:T(8,128)} %fusion.22, bf16[512,2048]{1,0:T(8,128)(2,1)} %param.13, bf16[384,512]{1,0:T(8,128)(2,1)} %reduce-scatter.4.cloned.1.call-done, f32[384]{0:T(512)S(1)} %convert_element_type.103), kind=kOutput, calls=%fused_computation.23 | convolution fusion | flops 807469056 | bytes 7210496 | tf_op jit(solution)/shard_map/dot_general | solution.py:70
  147.3 0.3 reduce-scatter.8.cloned.1.call-start
  147.7 0.9 select_n.45
  148.6 2.5 slice_reduce_fusion.14
  151.1 23.4 %reduce-scatter.6.cloned.1.call-done = bf16[384,512]{1,0:T(8,128)(2,1)} async-done(((bf16[384,2048]{1,0:T(8,128)(2,1)}), bf16[384,512]{1,0:T(8,128)(2,1)}) %reduce-scatter.6.cloned.1.call-update) | async-done | bytes 393232 | tf_op jit(solution)/shard_map/reduce_scatter | solution.py:72
  174.6 1.0 broadcast_maximum_fusion
  175.6 4.7 %convolution_divide_fusion = f32[2048,256]{1,0:T(8,128)} fusion(s32[2048]{0:T(1024)S(1)} %get-tuple-element.16, s32[2048]{0:T(1024)S(1)} %get-tuple-element.17, s32[2048]{0:T(1024)S(1)} %get-tuple-element.18, s32[2048]{0:T(1024)S(1)} %get-tuple-element.19, s32[2048]{0:T(1024)S(1)} %get-tuple-element.15, bf16[512,256]{1,0:T(8,128)(2,1)S(1)} %copy-done.4, ...), kind=kOutput, calls=%fused_computation.30 | convolution fusion | flops 515932160 | bytes 2801664 | tf_op jit(solution)/shard_map/dot_general | solution.py:78
  180.3 1.9 fusion.17
  182.2 138.5 %reduce-scatter.8.cloned.1.call-done = f32[64,256]{1,0:T(8,128)} async-done(((f32[2048,256]{1,0:T(8,128)}), f32[64,256]{1,0:T(8,128)}) %reduce-scatter.8.cloned.1.call-update) | async-done | bytes 65552 | tf_op jit(solution)/shard_map/reduce_scatter | solution.py:83
  320.7 0.9 multiply_reduce_fusion
  321.7 1.5 multiply_convert_fusion
  (28 shorter events, 0.8 us)
Async XLA Ops:
  6.5 59.2 %copy-start = (bf16[512,2048]{1,0:T(8,128)(2,1)S(1)}, bf16[512,2048]{1,0:T(8,128)(2,1)}, u32[]{:S(2)}) copy-start(bf16[512,2048]{1,0:T(8,128)(2,1)} %param.12) | copy-start | bytes 6291460
  6.5 135.9 %reduce-scatter.4.cloned.1.call-start = ((), (), s32[]{:S(2)}) async-start(), calls=%async_computation.3 | async-start | bytes 3538944 | tf_op jit(solution)/shard_map/reduce_scatter | solution.py:65
  9.5 7.5 %collective-permute-start = (s32[1,5376]{1,0:T(1,128)S(1)}, s32[1,5376]{1,0:T(1,128)S(1)}, u32[]{:S(2)}, u32[]{:S(2)}) collective-permute-start(s32[1,5376]{1,0:T(1,128)S(1)} %reshape.55), channel_id=1, source_target_pairs={{0,28},{4,0},{8,4},{12,8},{16,12},{20,16},{24,20},{28,24},{1,29},{... | collective-permute-start | bytes 64520 | tf_op jit(solution)/shard_map/ppermute | solution.py:45
  17.1 4.1 %collective-permute-start.1 = (s32[2,5376]{1,0:T(2,128)S(1)}, s32[2,5376]{1,0:T(2,128)S(1)}, u32[]{:S(2)}, u32[]{:S(2)}) collective-permute-start(s32[2,5376]{1,0:T(2,128)S(1)} %pad_add_fusion.1), channel_id=1, source_target_pairs={{0,24},{4,28},{8,0},{12,4},{16,8},{20,12},{24,16},{28,20},{1,25},{... | collective-permute-start | bytes 129032 | tf_op jit(solution)/shard_map/ppermute | solution.py:45
  21.2 6.4 %collective-permute-start.2 = (s32[4,5376]{1,0:T(4,128)S(1)}, s32[4,5376]{1,0:T(4,128)S(1)}, u32[]{:S(2)}, u32[]{:S(2)}) collective-permute-start(s32[4,5376]{1,0:T(4,128)S(1)} %pad_add_fusion), channel_id=1, source_target_pairs={{0,16},{4,20},{8,24},{12,28},{16,0},{20,4},{24,8},{28,12},{1,17},{... | collective-permute-start | bytes 258056 | tf_op jit(solution)/shard_map/ppermute | solution.py:45
  37.7 7.9 %copy-start.2 = (bf16[1024,512]{1,0:T(8,128)(2,1)S(1)}, bf16[1024,512]{1,0:T(8,128)(2,1)}, u32[]{:S(2)}) copy-start(bf16[1024,512]{1,0:T(8,128)(2,1)} %param.10) | copy-start | bytes 3145732
  37.7 7.9 %copy-start.5 = (bf16[4,512]{1,0:T(4,128)(2,1)S(1)}, bf16[4,512]{1,0:T(4,128)(2,1)}, u32[]{:S(2)}) copy-start(bf16[4,512]{1,0:T(4,128)(2,1)} %param.11) | copy-start | bytes 12292
  65.0 0.7 copy-start.3
  65.1 109.5 %reduce-scatter.6.cloned.1.call-start = ((), (), s32[]{:S(2)}) async-start(), calls=%async_computation.4 | async-start | bytes 1966080 | tf_op jit(solution)/shard_map/reduce_scatter | solution.py:72
  147.3 173.5 %reduce-scatter.8.cloned.1.call-start = ((), (), s32[]{:S(2)}) async-start(), calls=%async_computation.5 | async-start | bytes 2162688 | tf_op jit(solution)/shard_map/reduce_scatter | solution.py:83
  148.6 27.0 %copy-start.4 = (bf16[512,256]{1,0:T(8,128)(2,1)S(1)}, bf16[512,256]{1,0:T(8,128)(2,1)}, u32[]{:S(2)}) copy-start(bf16[512,256]{1,0:T(8,128)(2,1)} %param.15) | copy-start | bytes 786436
  175.6 4.7 %copy-start.1 = (bf16[512,256]{1,0:T(8,128)(2,1)S(1)}, bf16[512,256]{1,0:T(8,128)(2,1)}, u32[]{:S(2)}) copy-start(bf16[512,256]{1,0:T(8,128)(2,1)} %param.14) | copy-start | bytes 786436
Sparse Core Ops, SparseCore 0:
  65.2 77.1 reduce-scatter.3
  147.4 27.1 reduce-scatter.5
  182.3 138.3 reduce-scatter.7
